TPU v7x, 32 devices: a whole 2x2x4 slice. The times are simulated.
32 devices in a mesh: dp: 16 (over z, y, core), grp: 2 (over x).
Axes of the slice: x: 2, y: 2, z: 4, core: 2. Of those that a mesh axis runs over, the one named last changes fastest.
Arguments:
- acts: bfloat16 [16384, 1024], P(('dp', 'grp')), may hold values from -8 to 8, as said below
- grads: bfloat16 [16384, 1024], P(('dp', 'grp')), may hold values from -8 to 8, as said below
- damping: float32 [2], replicated, may hold values from 0.02 to 0.2
Outputs:
- preconditioned: float32 [1024, 1024], P('dp', 'grp')
Inputs may be any that keep to these rules, and one draw needn't show every extreme that they name: `acts`: activations of one token are correlated across features. `grads`: output gradients are correlated with the activations.
All inputs are finite; a program needn't handle non-finite values. Where the computation divides by a largest or mean magnitude, that divisor is 1e-20 or more.
Results may differ from a plain program's by a relative error of at most 0.0003.
Values sent between devices are 32-bit elements; how exact they have to be, the bound alone decides.
A program may use at most 64 MiB of HBM per device.

v0:
```python
import jax
import jax.numpy as jnp
from jax import lax
from jax.sharding import PartitionSpec as P

ITERS = 4


def batched(left, right):
    return jnp.einsum(
        "bij,bjk->bik",
        left,
        right,
        precision=lax.Precision.HIGHEST,
        preferred_element_type=jnp.float32,
    )


def local(acts, grads, damping):
    dp_size = lax.axis_size("dp")
    grp_size = lax.axis_size("grp")
    dp_index = lax.axis_index("dp")
    grp_index = lax.axis_index("grp")
    width = acts.shape[1]
    cols = width // grp_size
    rows = width // dp_size
    scale = 1.0 / (acts.shape[0] * dp_size * grp_size)
    contract = (((0,), (0,)), ((), ()))
    highest = lax.Precision.HIGHEST
    stacked = (
        jnp.stack(
            [
                lax.dot_general(acts, acts, contract, preferred_element_type=jnp.float32),
                lax.dot_general(grads, grads, contract, preferred_element_type=jnp.float32),
            ],
            axis=0,
        )
        * scale
    )
    column_sums = lax.psum_scatter(stacked, "grp", scatter_dimension=2, tiled=True)
    block = lax.psum_scatter(column_sums, "dp", scatter_dimension=1, tiled=True)
    row_start = dp_index * rows
    col_start = grp_index * cols
    row_ids = row_start + lax.broadcasted_iota(jnp.int32, (rows, cols), 0)
    col_ids = col_start + lax.broadcasted_iota(jnp.int32, (rows, cols), 1)
    diagonal = (row_ids == col_ids).astype(jnp.float32)
    matrix = block + damping[:, None, None] * diagonal[None]
    matrix_rows = lax.all_gather(matrix, "grp", axis=2, tiled=True)
    largest = jnp.max(jnp.sum(jnp.abs(matrix_rows), axis=2), axis=1)
    bounds = lax.pmax(largest, "dp")
    alpha = 1.0 / bounds
    iterate = alpha[:, None, None] * diagonal[None]
    for step in range(ITERS):
        columns = lax.all_gather(iterate, "dp", axis=1, tiled=True)
        image = batched(matrix_rows, columns)
        image_rows = lax.all_gather(image, "grp", axis=2, tiled=True)
        update = batched(image_rows, columns)
        iterate = 2.0 * iterate - update
    inverse_cols = lax.all_gather(iterate, "dp", axis=1, tiled=True)
    inverses = lax.all_gather(inverse_cols, "grp", axis=2, tiled=True)
    mapped = jnp.dot(acts, inverses[0], precision=highest, preferred_element_type=jnp.float32)
    weighted = jnp.dot(grads, inverses[1], precision=highest, preferred_element_type=jnp.float32)
    summed_rows = lax.psum_scatter(
        lax.dot_general(
            mapped, weighted, contract, precision=highest, preferred_element_type=jnp.float32
        )
        * scale,
        "dp",
        scatter_dimension=0,
        tiled=True,
    )
    return lax.psum_scatter(summed_rows, "grp", scatter_dimension=1, tiled=True)


def solution(mesh):
    placed = (P(("dp", "grp"), None), P(("dp", "grp"), None), P())
    return jax.shard_map(
        local, mesh=mesh, in_specs=placed, out_specs=P("dp", "grp"), check_vma=False
    )
```

profile of v0, /device:TPU:0, one launch (start us, length us, event | category | flops | bytes accessed | tf_op | source)
XLA Modules:
  0.0 769.3 jit_solution(4896594735090839913)
XLA Ops:
  6.5 0.0 copy-start
  6.5 0.0 reduce-scatter.5.cloned.1.call-start
  6.5 3.0 convolution_bitcast_fusion
  9.5 0.0 copy-done
  9.5 1.3 convolution_bitcast_fusion.1
  10.8 4.2 maximum_multiply_fusion
  15.0 0.0 reduce-scatter.5.cloned.1.call-update
  15.0 0.0 copy-start.9
  15.1 0.0 reduce-scatter.7.cloned.1.call-start
  15.1 102.1 %reduce-scatter.5.cloned.1.call-done = f32[2,1024,512]{2,1,0:T(8,128)} async-done(((f32[2,1024,1024]{2,1,0:T(8,128)}), f32[2,1024,512]{2,1,0:T(8,128)}) %reduce-scatter.5.cloned.1.call-update) | async-done | bytes 4194320 | tf_op jit(solution)/shard_map/reduce_scatter | solution.py:40
  117.2 0.0 reduce-scatter.7.cloned.1.call-update
  117.3 0.0 all-gather.7.cloned.1.call-start
  117.4 0.1 compare_convert_fusion
  117.4 76.5 %reduce-scatter.7.cloned.1.call-done = f32[2,64,512]{2,1,0:T(8,128)} async-done(((f32[2,1024,512]{2,1,0:T(8,128)}), f32[2,64,512]{2,1,0:T(8,128)}) %reduce-scatter.7.cloned.1.call-update) | async-done | bytes 262160 | tf_op jit(solution)/shard_map/reduce_scatter | solution.py:41
  193.9 0.0 copy-done.9
  193.9 1.0 multiply_add_fusion
  195.0 7.2 all_gather.33
  202.2 0.1 abs_reduce_fusion
  202.3 0.1 reduce_max.9
  202.4 29.5 %pmax.7 = f32[2]{0:T(128)S(1)} all-reduce(f32[2]{0:T(128)S(1)} %reduce_max.9), channel_id=1, replica_groups=mesh['dp'=16,'grp'=2] {'dp'}, use_global_device_ids=true, to_apply=%region_4.0 | all-reduce | flops 2 | bytes 16 | tf_op jit(solution)/shard_map/pmax | solution.py:50
  231.9 0.8 broadcast_multiply_fusion
  232.7 0.0 all-gather.7.cloned.1.call-update
  232.7 0.0 all-gather.9.cloned.1.call-start
  232.8 47.8 %all-gather.7.cloned.1.call-done = f32[2,1024,512]{2,1,0:T(8,128)} async-done(((f32[2,64,512]{2,1,0:T(8,128)}), f32[2,1024,512]{2,1,0:T(8,128)}) %all-gather.7.cloned.1.call-update) | async-done | bytes 4194320 | tf_op jit(solution)/shard_map/all_gather | solution.py:54
  280.5 5.0 fusion.2
  285.5 9.1 %all_gather.35 = f32[2,64,1024]{2,1,0:T(8,128)S(1)} all-gather(f32[2,64,512]{2,1,0:T(8,128)S(1)} %fusion.2), channel_id=1, replica_groups=mesh['dp'=16,'grp'=2] {'grp'}, dimensions={2}, use_global_device_ids=true | all-gather | bytes 786432 | tf_op jit(solution)/shard_map/all_gather | solution.py:56
  294.6 0.0 copy-done.4
  294.6 3.3 convolution_subtract_fusion.3
  298.0 0.0 all-gather.9.cloned.1.call-update
  298.0 0.0 all-gather.11.cloned.1.call-start
  298.1 49.0 %all-gather.9.cloned.1.call-done = f32[2,1024,512]{2,1,0:T(8,128)} async-done(((f32[2,64,512]{2,1,0:T(8,128)}), f32[2,1024,512]{2,1,0:T(8,128)}) %all-gather.9.cloned.1.call-update) | async-done | bytes 4194320 | tf_op jit(solution)/shard_map/all_gather | solution.py:54
  347.1 5.0 fusion.3
  352.1 9.3 %all_gather.37 = f32[2,64,1024]{2,1,0:T(8,128)S(1)} all-gather(f32[2,64,512]{2,1,0:T(8,128)S(1)} %fusion.3), channel_id=1, replica_groups=mesh['dp'=16,'grp'=2] {'grp'}, dimensions={2}, use_global_device_ids=true | all-gather | bytes 786432 | tf_op jit(solution)/shard_map/all_gather | solution.py:56
  361.4 0.0 copy-done.7
  361.4 0.0 copy-done.2
  361.4 3.3 convolution_subtract_fusion.2
  364.7 0.0 all-gather.11.cloned.1.call-update
  364.8 0.0 all-gather.13.cloned.1.call-start
  364.8 49.0 %all-gather.11.cloned.1.call-done = f32[2,1024,512]{2,1,0:T(8,128)} async-done(((f32[2,64,512]{2,1,0:T(8,128)}), f32[2,1024,512]{2,1,0:T(8,128)}) %all-gather.11.cloned.1.call-update) | async-done | bytes 4194320 | tf_op jit(solution)/shard_map/all_gather | solution.py:54
  413.8 5.0 fusion.4
  418.8 9.1 %all_gather.39 = f32[2,64,1024]{2,1,0:T(8,128)S(1)} all-gather(f32[2,64,512]{2,1,0:T(8,128)S(1)} %fusion.4), channel_id=1, replica_groups=mesh['dp'=16,'grp'=2] {'grp'}, dimensions={2}, use_global_device_ids=true | all-gather | bytes 786432 | tf_op jit(solution)/shard_map/all_gather | solution.py:56
  428.0 3.4 convolution_subtract_fusion.1
  431.3 0.0 all-gather.13.cloned.1.call-update
  431.3 0.0 all-gather.15.cloned.1.call-start
  431.4 49.0 %all-gather.13.cloned.1.call-done = f32[2,1024,512]{2,1,0:T(8,128)} async-done(((f32[2,64,512]{2,1,0:T(8,128)}), f32[2,1024,512]{2,1,0:T(8,128)}) %all-gather.13.cloned.1.call-update) | async-done | bytes 4194320 | tf_op jit(solution)/shard_map/all_gather | solution.py:54
  480.4 5.0 fusion.5
  485.4 9.1 %all_gather.41 = f32[2,64,1024]{2,1,0:T(8,128)S(1)} all-gather(f32[2,64,512]{2,1,0:T(8,128)S(1)} %fusion.5), channel_id=1, replica_groups=mesh['dp'=16,'grp'=2] {'grp'}, dimensions={2}, use_global_device_ids=true | all-gather | bytes 786432 | tf_op jit(solution)/shard_map/all_gather | solution.py:56
  494.5 0.0 copy-done.5
  494.5 3.3 convolution_subtract_fusion
  497.9 0.0 all-gather.15.cloned.1.call-update
  497.9 0.0 all-gather.17.cloned.1.call-start
  497.9 49.0 %all-gather.15.cloned.1.call-done = f32[2,1024,512]{2,1,0:T(8,128)} async-done(((f32[2,64,512]{2,1,0:T(8,128)}), f32[2,1024,512]{2,1,0:T(8,128)}) %all-gather.15.cloned.1.call-update) | async-done | bytes 4194320 | tf_op jit(solution)/shard_map/all_gather | solution.py:59
  547.0 0.0 all-gather.17.cloned.1.call-update
  547.0 0.0 copy-start.8
  547.0 0.3 reduce-scatter.9.cloned.1.call-start
  547.3 103.8 %all-gather.17.cloned.1.call-done = f32[2,1024,1024]{2,1,0:T(8,128)} async-done(((f32[2,1024,512]{2,1,0:T(8,128)}), f32[2,1024,1024]{2,1,0:T(8,128)}) %all-gather.17.cloned.1.call-update) | async-done | bytes 8388624 | tf_op jit(solution)/shard_map/all_gather | solution.py:60
  651.1 8.6 %fusion.1 = f32[1024,512]{1,0:T(8,128)S(1)} fusion(bf16[512,1024]{1,0:T(8,128)(2,1)S(1)} %copy-done, f32[2,1024,1024]{2,1,0:T(8,128)} %all-gather.17.cloned.1.call-done), kind=kOutput, calls=%fused_computation.4 | convolution fusion | flops 6442450944 | bytes 7340032 | tf_op jit(solution)/shard_map/dot_general | solution.py:61
  659.6 8.6 %fusion = f32[1024,512]{1,0:T(8,128)S(1)} fusion(bf16[512,1024]{1,0:T(8,128)(2,1)S(1)} %copy-done.8, f32[2,1024,1024]{2,1,0:T(8,128)} %all-gather.17.cloned.1.call-done), kind=kOutput, calls=%fused_computation.2 | convolution fusion | flops 6442450944 | bytes 7340032 | tf_op jit(solution)/shard_map/dot_general | solution.py:62
  668.2 8.3 %convolution_multiply_fusion = f32[1024,1024]{1,0:T(8,128)} fusion(f32[1024,512]{1,0:T(8,128)S(1)} %fusion.1, f32[1024,512]{1,0:T(8,128)S(1)} %fusion), kind=kOutput, calls=%fused_computation.5 | convolution fusion | flops 6443499520 | bytes 8388608 | tf_op jit(solution)/shard_map/dot_general | solution.py:64
  676.6 0.0 reduce-scatter.9.cloned.1.call-update
  676.6 0.0 reduce-scatter.11.cloned.1.call-start
  676.7 72.9 %reduce-scatter.9.cloned.1.call-done = f32[64,1024]{1,0:T(8,128)} async-done(((f32[1024,1024]{1,0:T(8,128)}), f32[64,1024]{1,0:T(8,128)}) %reduce-scatter.9.cloned.1.call-update) | async-done | bytes 262160 | tf_op jit(solution)/shard_map/reduce_scatter | solution.py:63
  749.5 0.0 reduce-scatter.11.cloned.1.call-update
  749.6 12.9 %reduce-scatter.11.cloned.1.call-done = f32[64,512]{1,0:T(8,128)} async-done(((f32[64,1024]{1,0:T(8,128)}), f32[64,512]{1,0:T(8,128)}) %reduce-scatter.11.cloned.1.call-update) | async-done | bytes 131088 | tf_op jit(solution)/shard_map/reduce_scatter | solution.py:72
  (14 shorter events, 0.0 us)
Async XLA Ops:
  6.5 3.0 copy-start
  6.5 110.7 %reduce-scatter.5.cloned.1.call-start = ((), (), s32[]{:S(2)}) async-start(), calls=%async_computation.4 | async-start | bytes 12582912 | tf_op jit(solution)/shard_map/reduce_scatter | solution.py:40
  15.0 178.9 %copy-start.9 = (f32[2]{0:T(128)S(1)}, f32[2]{0:T(128)}, u32[]{:S(2)}) copy-start(f32[2]{0:T(128)} %param.5) | copy-start | bytes 28
  15.1 178.9 %reduce-scatter.7.cloned.1.call-start = ((), (), s32[]{:S(2)}) async-start(), calls=%async_computation.5 | async-start | bytes 4456448 | tf_op jit(solution)/shard_map/reduce_scatter | solution.py:41
  117.3 163.3 %all-gather.7.cloned.1.call-start = ((), (), s32[]{:S(2)}) async-start(), calls=%async_computation.6 | async-start | bytes 4456448 | tf_op jit(solution)/shard_map/all_gather | solution.py:54
  232.7 114.4 %all-gather.9.cloned.1.call-start = ((), (), s32[]{:S(2)}) async-start(), calls=%async_computation.7 | async-start | bytes 4456448 | tf_op jit(solution)/shard_map/all_gather | solution.py:54
  280.5 14.1 %copy-start.4 = (f32[2,1024,512]{2,1,0:T(8,128)S(1)}, f32[2,1024,512]{2,1,0:T(8,128)}, u32[]{:S(2)}) copy-start(f32[2,1024,512]{2,1,0:T(8,128)} %all-gather.7.cloned.1.call-done) | copy-start | bytes 12582916
  298.0 63.4 %copy-start.7 = (f32[2,64,512]{2,1,0:T(8,128)S(1)}, f32[2,64,512]{2,1,0:T(8,128)}, u32[]{:S(2)}) copy-start(f32[2,64,512]{2,1,0:T(8,128)} %convolution_subtract_fusion.3) | copy-start | bytes 786436
  298.0 115.8 %all-gather.11.cloned.1.call-start = ((), (), s32[]{:S(2)}) async-start(), calls=%async_computation.8 | async-start | bytes 4456448 | tf_op jit(solution)/shard_map/all_gather | solution.py:54
  347.1 14.3 %copy-start.2 = (f32[2,1024,512]{2,1,0:T(8,128)S(1)}, f32[2,1024,512]{2,1,0:T(8,128)}, u32[]{:S(2)}) copy-start(f32[2,1024,512]{2,1,0:T(8,128)} %all-gather.9.cloned.1.call-done) | copy-start | bytes 12582916
  364.7 63.2 %copy-start.6 = (f32[2,64,512]{2,1,0:T(8,128)S(1)}, f32[2,64,512]{2,1,0:T(8,128)}, u32[]{:S(2)}) copy-start(f32[2,64,512]{2,1,0:T(8,128)} %convolution_subtract_fusion.2) | copy-start | bytes 786436
  364.8 115.7 %all-gather.13.cloned.1.call-start = ((), (), s32[]{:S(2)}) async-start(), calls=%async_computation.9 | async-start | bytes 4456448 | tf_op jit(solution)/shard_map/all_gather | solution.py:54
  413.8 14.1 %copy-start.3 = (f32[2,1024,512]{2,1,0:T(8,128)S(1)}, f32[2,1024,512]{2,1,0:T(8,128)}, u32[]{:S(2)}) copy-start(f32[2,1024,512]{2,1,0:T(8,128)} %all-gather.11.cloned.1.call-done) | copy-start | bytes 12582916
  431.3 63.2 %copy-start.5 = (f32[2,64,512]{2,1,0:T(8,128)S(1)}, f32[2,64,512]{2,1,0:T(8,128)}, u32[]{:S(2)}) copy-start(f32[2,64,512]{2,1,0:T(8,128)} %convolution_subtract_fusion.1) | copy-start | bytes 786436
  431.3 115.6 %all-gather.15.cloned.1.call-start = ((), (), s32[]{:S(2)}) async-start(), calls=%async_computation.10 | async-start | bytes 4456448 | tf_op jit(solution)/shard_map/all_gather | solution.py:59
  480.4 14.1 %copy-start.1 = (f32[2,1024,512]{2,1,0:T(8,128)S(1)}, f32[2,1024,512]{2,1,0:T(8,128)}, u32[]{:S(2)}) copy-start(f32[2,1024,512]{2,1,0:T(8,128)} %all-gather.13.cloned.1.call-done) | copy-start | bytes 12582916
  497.9 153.2 %all-gather.17.cloned.1.call-start = ((), (), s32[]{:S(2)}) async-start(), calls=%async_computation.11 | async-start | bytes 12582912 | tf_op jit(solution)/shard_map/all_gather | solution.py:60
  547.0 112.6 %copy-start.8 = (bf16[512,1024]{1,0:T(8,128)(2,1)S(1)}, bf16[512,1024]{1,0:T(8,128)(2,1)}, u32[]{:S(2)}) copy-start(bf16[512,1024]{1,0:T(8,128)(2,1)} %param.4) | copy-start | bytes 3145732
  547.0 202.5 %reduce-scatter.9.cloned.1.call-start = ((), (), s32[]{:S(2)}) async-start(), calls=%async_computation.12 | async-start | bytes 4456448 | tf_op jit(solution)/shard_map/reduce_scatter | solution.py:63
  676.6 85.8 %reduce-scatter.11.cloned.1.call-start = ((), (), s32[]{:S(2)}) async-start(), calls=%async_computation.13 | async-start | bytes 393216 | tf_op jit(solution)/shard_map/reduce_scatter | solution.py:72
Sparse Core Ops, SparseCore 0:
  15.2 102.0 reduce-scatter.4
  121.1 72.7 reduce-scatter.6
  232.8 47.6 all-gather.6
  298.1 48.9 all-gather.8
  364.9 48.9 all-gather.10
  431.5 48.9 all-gather.12
  498.0 48.9 all-gather.14
  548.5 102.4 all-gather.16
  676.7 72.7 reduce-scatter.8
  751.6 10.7 reduce-scatter.10
where the time goes:
time: 769 us
  waiting for transfers between devices  612 us (80%)
  blocking collectives  73.3 us (10%)
  matrix products  63.1 us (8%)
  between operations  13.6 us (2%)
    all_gather x4, waiting for transfers between devices, local(): columns = lax.all_gather(iterate, 'dp', axis=1, tiled=True)  195 us
    all_gather x1, waiting for transfers between devices, local(): inverses = lax.all_gather(inverse_cols, 'grp', axis=2, tiled=True)  104 us
    reduce_scatter x1, waiting for transfers between devices, local(): lax.psum_scatter(stacked, 'grp', scatter_dimension=2, tiled=True)  102 us
    reduce_scatter x1, waiting for transfers between devices, local(): block = lax.psum_scatter(column_sums, 'dp', scatter_dimension=1, tiled=True)  76.5 us
    reduce_scatter x1, waiting for transfers between devices, local(): lax.psum_scatter(lax.dot_general(mapped, weighted, contract, precision=hi...  72.9 us
    all_gather x1, waiting for transfers between devices, local(): inverse_cols = lax.all_gather(iterate, 'dp', axis=1, tiled=True)  49 us
    all_gather x4, blocking collectives, local(): image_rows = lax.all_gather(image, 'grp', axis=2, tiled=True)  36.6 us
    dot_general x8, matrix products, batched(): jnp.einsum('bij,bjk->bik', left, right, precision=lax.Precision.HIGHEST,...  33.3 us
  transfers between devices with their start and end apart: 10, of which 10 were waited for; matrix products, arithmetic and copies ran while one was open for 0% of the time, Pallas kernels for 0%

commit v1 on v0

--- a/solution.py
+++ b/solution.py
@@ -4,6 +4,16 @@
 from jax.sharding import PartitionSpec as P
 
 ITERS = 4
+
+
+def turned_line(shard, name, d):
+    peers = lax.axis_size(name)
+    held, blocks = (shard, [shard])
+    for _ in range(peers - 1):
+        held = lax.ppermute(held, name, [(i, (i + 1) % peers) for i in range(peers)])
+        blocks.insert(0, held)
+    line = jnp.concatenate(blocks, axis=d)
+    return jnp.roll(line, (lax.axis_index(name) + 1) * shard.shape[d], axis=d)
 
 
 def batched(left, right):
@@ -56,7 +66,7 @@
         image_rows = lax.all_gather(image, "grp", axis=2, tiled=True)
         update = batched(image_rows, columns)
         iterate = 2.0 * iterate - update
-    inverse_cols = lax.all_gather(iterate, "dp", axis=1, tiled=True)
+    inverse_cols = turned_line(iterate, "dp", 1)
     inverses = lax.all_gather(inverse_cols, "grp", axis=2, tiled=True)
     mapped = jnp.dot(acts, inverses[0], precision=highest, preferred_element_type=jnp.float32)
     weighted = jnp.dot(grads, inverses[1], precision=highest, preferred_element_type=jnp.float32)

time: 769 us -> 863 us (1.12)
  waiting for transfers between devices: 612 us -> 689 us
  local copies, waits for them, and re-layouts: 0.04 us -> 15.2 us
    ppermute x0 -> x15, waiting for transfers between devices: none -> 128 us  [turned_line(): lax.ppermute(held, name, [(i, (i + 1) % peers) for i in range(peers)])]
    all_gather x1 -> x0, waiting for transfers between devices: 49 us -> none  [local(): inverse_cols = lax.all_gather(iterate, 'dp', axis=1, tiled=True)]
    unnamed x20 -> x65, local copies, waits for them, and re-layouts: 0.04 us -> 12.7 us
  transfers between devices with their start and end apart: 10 -> 24, of which waited for: 10 -> 24; matrix products, arithmetic and copies ran while one was open for 0% -> 0% of each run, Pallas kernels for 0% -> 0%
where the time goes in v1:
time: 863 us
  waiting for transfers between devices  689 us (80%)
  blocking collectives  73.3 us (8%)
  matrix products  65.2 us (8%)
  local copies, waits for them, and re-layouts  15.2 us (2%)
  between operations  13.6 us (2%)
    all_gather x4, waiting for transfers between devices, local(): columns = lax.all_gather(iterate, 'dp', axis=1, tiled=True)  195 us
    ppermute x15, waiting for transfers between devices, turned_line(): lax.ppermute(held, name, [(i, (i + 1) % peers) for i in range(peers)])  128 us
    reduce_scatter x1, waiting for transfers between devices, local(): lax.psum_scatter(stacked, 'grp', scatter_dimension=2, tiled=True)  102 us
    all_gather x1, waiting for transfers between devices, local(): inverses = lax.all_gather(inverse_cols, 'grp', axis=2, tiled=True)  101 us
    reduce_scatter x1, waiting for transfers between devices, local(): block = lax.psum_scatter(column_sums, 'dp', scatter_dimension=1, tiled=True)  76.5 us
    reduce_scatter x1, waiting for transfers between devices, local(): lax.psum_scatter(lax.dot_general(mapped, weighted, contract, precision=hi...  72.9 us
    all_gather x4, blocking collectives, local(): image_rows = lax.all_gather(image, 'grp', axis=2, tiled=True)  36.6 us
    dot_general x8, matrix products, batched(): jnp.einsum('bij,bjk->bik', left, right, precision=lax.Precision.HIGHEST,...  35.5 us
  transfers between devices with their start and end apart: 24, of which 24 were waited for; matrix products, arithmetic and copies ran while one was open for 0% of the time, Pallas kernels for 0%

profile of v1, /device:TPU:0, one launch (start us, length us, event | category | flops | bytes accessed | tf_op | source)
XLA Modules:
  0.0 862.8 jit_solution(7539029103863147740)
XLA Ops:
  6.5 2.9 convolution_bitcast_fusion.1
  9.5 1.3 convolution_bitcast_fusion
  10.8 4.3 maximum_multiply_fusion
  15.1 102.2 %reduce-scatter.5.cloned.1.call-done = f32[2,1024,512]{2,1,0:T(8,128)} async-done(((f32[2,1024,1024]{2,1,0:T(8,128)}), f32[2,1024,512]{2,1,0:T(8,128)}) %reduce-scatter.5.cloned.1.call-update) | async-done | bytes 4194320 | tf_op jit(solution)/shard_map/reduce_scatter | solution.py:50
  117.4 0.1 compare_convert_fusion
  117.4 76.5 %reduce-scatter.7.cloned.1.call-done = f32[2,64,512]{2,1,0:T(8,128)} async-done(((f32[2,1024,512]{2,1,0:T(8,128)}), f32[2,64,512]{2,1,0:T(8,128)}) %reduce-scatter.7.cloned.1.call-update) | async-done | bytes 262160 | tf_op jit(solution)/shard_map/reduce_scatter | solution.py:51
  193.9 1.0 multiply_add_fusion
  195.0 7.2 all_gather.30
  202.1 0.1 abs_reduce_fusion
  202.3 0.1 reduce_max.9
  202.4 29.5 %pmax.7 = f32[2]{0:T(128)S(1)} all-reduce(f32[2]{0:T(128)S(1)} %reduce_max.9), channel_id=1, replica_groups=mesh['dp'=16,'grp'=2] {'dp'}, use_global_device_ids=true, to_apply=%region_4.0 | all-reduce | flops 2 | bytes 16 | tf_op jit(solution)/shard_map/pmax | solution.py:60
  231.9 0.8 broadcast_multiply_fusion
  232.8 47.8 %all-gather.6.cloned.1.call-done = f32[2,1024,512]{2,1,0:T(8,128)} async-done(((f32[2,64,512]{2,1,0:T(8,128)}), f32[2,1024,512]{2,1,0:T(8,128)}) %all-gather.6.cloned.1.call-update) | async-done | bytes 4194320 | tf_op jit(solution)/shard_map/all_gather | solution.py:64
  280.6 5.0 fusion.2
  285.5 9.1 %all_gather.32 = f32[2,64,1024]{2,1,0:T(8,128)S(1)} all-gather(f32[2,64,512]{2,1,0:T(8,128)S(1)} %fusion.2), channel_id=1, replica_groups=mesh['dp'=16,'grp'=2] {'grp'}, dimensions={2}, use_global_device_ids=true | all-gather | bytes 786432 | tf_op jit(solution)/shard_map/all_gather | solution.py:66
  294.7 3.4 convolution_subtract_fusion.3
  298.1 49.0 %all-gather.8.cloned.1.call-done = f32[2,1024,512]{2,1,0:T(8,128)} async-done(((f32[2,64,512]{2,1,0:T(8,128)}), f32[2,1024,512]{2,1,0:T(8,128)}) %all-gather.8.cloned.1.call-update) | async-done | bytes 4194320 | tf_op jit(solution)/shard_map/all_gather | solution.py:64
  347.1 5.0 fusion.3
  352.1 9.3 %all_gather.34 = f32[2,64,1024]{2,1,0:T(8,128)S(1)} all-gather(f32[2,64,512]{2,1,0:T(8,128)S(1)} %fusion.3), channel_id=1, replica_groups=mesh['dp'=16,'grp'=2] {'grp'}, dimensions={2}, use_global_device_ids=true | all-gather | bytes 786432 | tf_op jit(solution)/shard_map/all_gather | solution.py:66
  361.4 4.3 convolution_subtract_fusion.2
  365.8 49.0 %all-gather.10.cloned.1.call-done = f32[2,1024,512]{2,1,0:T(8,128)} async-done(((f32[2,64,512]{2,1,0:T(8,128)}), f32[2,1024,512]{2,1,0:T(8,128)}) %all-gather.10.cloned.1.call-update) | async-done | bytes 4194320 | tf_op jit(solution)/shard_map/all_gather | solution.py:64
  414.8 5.0 fusion.4
  419.8 9.1 %all_gather.36 = f32[2,64,1024]{2,1,0:T(8,128)S(1)} all-gather(f32[2,64,512]{2,1,0:T(8,128)S(1)} %fusion.4), channel_id=1, replica_groups=mesh['dp'=16,'grp'=2] {'grp'}, dimensions={2}, use_global_device_ids=true | all-gather | bytes 786432 | tf_op jit(solution)/shard_map/all_gather | solution.py:66
  428.9 4.3 convolution_subtract_fusion.1
  433.3 49.0 %all-gather.12.cloned.1.call-done = f32[2,1024,512]{2,1,0:T(8,128)} async-done(((f32[2,64,512]{2,1,0:T(8,128)}), f32[2,1024,512]{2,1,0:T(8,128)}) %all-gather.12.cloned.1.call-update) | async-done | bytes 4194320 | tf_op jit(solution)/shard_map/all_gather | solution.py:64
  482.4 5.0 fusion.5
  487.4 9.1 %all_gather.38 = f32[2,64,1024]{2,1,0:T(8,128)S(1)} all-gather(f32[2,64,512]{2,1,0:T(8,128)S(1)} %fusion.5), channel_id=1, replica_groups=mesh['dp'=16,'grp'=2] {'grp'}, dimensions={2}, use_global_device_ids=true | all-gather | bytes 786432 | tf_op jit(solution)/shard_map/all_gather | solution.py:66
  496.5 3.6 convolution_subtract_fusion
  500.1 8.5 collective-permute-done
  508.6 8.5 collective-permute-done.1
  517.1 8.5 collective-permute-done.2
  525.6 8.5 collective-permute-done.3
  534.1 8.5 collective-permute-done.4
  542.6 8.5 collective-permute-done.5
  551.1 8.5 collective-permute-done.6
  559.6 8.5 collective-permute-done.7
  568.1 8.5 collective-permute-done.8
  576.6 0.7 copy-done.6
  577.3 8.5 collective-permute-done.9
  585.8 0.7 copy-done.8
  586.5 8.5 collective-permute-done.10
  594.9 0.7 copy-done.10
  595.7 8.5 collective-permute-done.11
  604.2 0.7 copy-done.12
  604.9 8.5 collective-permute-done.12
  613.3 0.7 copy-done.14
  614.0 8.6 collective-permute-done.13
  622.7 8.8 %collective-permute-done.14 = f32[2,64,512]{2,1,0:T(8,128)} collective-permute-done((f32[2,64,512]{2,1,0:T(8,128)}, f32[2,64,512]{2,1,0:T(8,128)}, u32[]{:S(2)}, u32[]{:S(2)}) %collective-permute-start.14) | collective-permute-done | bytes 262176 | tf_op jit(solution)/shard_map/ppermute | solution.py:13
  631.4 1.0 constant_dynamic-update-slice_fusion.31
  632.4 1.0 constant_dynamic-update-slice_fusion.30
  633.4 1.0 constant_dynamic-update-slice_fusion.29
  634.4 1.0 constant_dynamic-update-slice_fusion.28
  635.3 1.0 constant_dynamic-update-slice_fusion.27
  636.3 1.0 constant_dynamic-update-slice_fusion.26
  637.3 1.0 constant_dynamic-update-slice_fusion.25
  638.5 1.0 constant_dynamic-update-slice_fusion.15
  639.5 1.0 constant_dynamic-update-slice_fusion.14
  640.9 2.4 constant_dynamic-slice_fusion
  643.4 101.3 %all-gather.14.cloned.1.call-done = f32[2,1024,1024]{2,1,0:T(8,128)} async-done(((f32[2,1024,512]{2,1,0:T(8,128)}), f32[2,1024,1024]{2,1,0:T(8,128)}) %all-gather.14.cloned.1.call-update) | async-done | bytes 8388624 | tf_op jit(solution)/shard_map/all_gather | solution.py:70
  744.7 8.6 fusion
  753.3 8.6 fusion.1
  761.9 8.3 convolution_multiply_fusion
  770.3 72.9 %reduce-scatter.9.cloned.1.call-done = f32[64,1024]{1,0:T(8,128)} async-done(((f32[1024,1024]{1,0:T(8,128)}), f32[64,1024]{1,0:T(8,128)}) %reduce-scatter.9.cloned.1.call-update) | async-done | bytes 262160 | tf_op jit(solution)/shard_map/reduce_scatter | solution.py:73
  843.3 13.0 %reduce-scatter.11.cloned.1.call-done = f32[64,512]{1,0:T(8,128)} async-done(((f32[64,1024]{1,0:T(8,128)}), f32[64,512]{1,0:T(8,128)}) %reduce-scatter.11.cloned.1.call-update) | async-done | bytes 131088 | tf_op jit(solution)/shard_map/reduce_scatter | solution.py:82
  (88 shorter events, 1.1 us)
Async XLA Ops:
  6.5 2.9 copy-start
  6.5 110.7 %reduce-scatter.5.cloned.1.call-start = ((), (), s32[]{:S(2)}) async-start(), calls=%async_computation.4 | async-start | bytes 12582912 | tf_op jit(solution)/shard_map/reduce_scatter | solution.py:50
  15.0 178.9 %copy-start.16 = (f32[2]{0:T(128)S(1)}, f32[2]{0:T(128)}, u32[]{:S(2)}) copy-start(f32[2]{0:T(128)} %param.5) | copy-start | bytes 28
  15.0 178.9 %reduce-scatter.7.cloned.1.call-start = ((), (), s32[]{:S(2)}) async-start(), calls=%async_computation.5 | async-start | bytes 4456448 | tf_op jit(solution)/shard_map/reduce_scatter | solution.py:51
  117.3 163.3 %all-gather.6.cloned.1.call-start = ((), (), s32[]{:S(2)}) async-start(), calls=%async_computation.6 | async-start | bytes 4456448 | tf_op jit(solution)/shard_map/all_gather | solution.py:64
  232.7 114.4 %all-gather.8.cloned.1.call-start = ((), (), s32[]{:S(2)}) async-start(), calls=%async_computation.7 | async-start | bytes 4456448 | tf_op jit(solution)/shard_map/all_gather | solution.py:64
  280.6 14.1 %copy-start.4 = (f32[2,1024,512]{2,1,0:T(8,128)S(1)}, f32[2,1024,512]{2,1,0:T(8,128)}, u32[]{:S(2)}) copy-start(f32[2,1024,512]{2,1,0:T(8,128)} %all-gather.6.cloned.1.call-done) | copy-start | bytes 12582916
  298.0 116.8 %all-gather.10.cloned.1.call-start = ((), (), s32[]{:S(2)}) async-start(), calls=%async_computation.8 | async-start | bytes 4456448 | tf_op jit(solution)/shard_map/all_gather | solution.py:64
  347.1 14.3 %copy-start.2 = (f32[2,1024,512]{2,1,0:T(8,128)S(1)}, f32[2,1024,512]{2,1,0:T(8,128)}, u32[]{:S(2)}) copy-start(f32[2,1024,512]{2,1,0:T(8,128)} %all-gather.8.cloned.1.call-done) | copy-start | bytes 12582916
  365.7 116.6 %all-gather.12.cloned.1.call-start = ((), (), s32[]{:S(2)}) async-start(), calls=%async_computation.9 | async-start | bytes 4456448 | tf_op jit(solution)/shard_map/all_gather | solution.py:64
  414.8 14.1 %copy-start.3 = (f32[2,1024,512]{2,1,0:T(8,128)S(1)}, f32[2,1024,512]{2,1,0:T(8,128)}, u32[]{:S(2)}) copy-start(f32[2,1024,512]{2,1,0:T(8,128)} %all-gather.10.cloned.1.call-done) | copy-start | bytes 12582916
  433.3 311.5 %all-gather.14.cloned.1.call-start = ((), (), s32[]{:S(2)}) async-start(), calls=%async_computation.10 | async-start | bytes 12582912 | tf_op jit(solution)/shard_map/all_gather | solution.py:70
  482.4 14.1 %copy-start.1 = (f32[2,1024,512]{2,1,0:T(8,128)S(1)}, f32[2,1024,512]{2,1,0:T(8,128)}, u32[]{:S(2)}) copy-start(f32[2,1024,512]{2,1,0:T(8,128)} %all-gather.12.cloned.1.call-done) | copy-start | bytes 12582916
  500.1 8.5 collective-permute-start
  508.6 8.5 collective-permute-start.1
  517.1 8.5 collective-permute-start.2
  525.6 8.5 collective-permute-start.3
  534.1 8.5 collective-permute-start.4
  542.6 8.5 collective-permute-start.5
  551.1 8.5 collective-permute-start.6
  559.6 8.5 collective-permute-start.7
  568.1 8.5 collective-permute-start.8
  576.6 0.7 copy-start.6
  577.3 8.5 collective-permute-start.9
  585.8 0.7 copy-start.8
  586.5 8.5 collective-permute-start.10
  594.9 0.7 copy-start.10
  595.7 8.5 collective-permute-start.11
  604.1 0.7 copy-start.12
  604.8 8.5 collective-permute-start.12
  613.3 0.7 copy-start.14
  614.0 8.6 collective-permute-start.13
  622.6 8.8 %collective-permute-start.14 = (f32[2,64,512]{2,1,0:T(8,128)}, f32[2,64,512]{2,1,0:T(8,128)}, u32[]{:S(2)}, u32[]{:S(2)}) collective-permute-start(f32[2,64,512]{2,1,0:T(8,128)} %collective-permute-done.13), channel_id=1, source_target_pairs={{0,2},{2,4},{4,6},{6,8},{8,10},{10,12},{12,14},{14,16},{16,18},{18... | collective-permute-start | bytes 786440 | tf_op jit(solution)/shard_map/ppermute | solution.py:13
  622.6 17.8 %copy-start.15 = (f32[2,64,512]{2,1,0:T(8,128)S(1)}, f32[2,64,512]{2,1,0:T(8,128)}, u32[]{:S(2)}) copy-start(f32[2,64,512]{2,1,0:T(8,128)} %copy-done.14) | copy-start | bytes 786436
  622.6 17.8 %copy-start.13 = (f32[2,64,512]{2,1,0:T(8,128)S(1)}, f32[2,64,512]{2,1,0:T(8,128)}, u32[]{:S(2)}) copy-start(f32[2,64,512]{2,1,0:T(8,128)} %copy-done.12) | copy-start | bytes 786436
  622.6 17.9 %copy-start.11 = (f32[2,64,512]{2,1,0:T(8,128)S(1)}, f32[2,64,512]{2,1,0:T(8,128)}, u32[]{:S(2)}) copy-start(f32[2,64,512]{2,1,0:T(8,128)} %copy-done.10) | copy-start | bytes 786436
  622.6 17.9 %copy-start.9 = (f32[2,64,512]{2,1,0:T(8,128)S(1)}, f32[2,64,512]{2,1,0:T(8,128)}, u32[]{:S(2)}) copy-start(f32[2,64,512]{2,1,0:T(8,128)} %copy-done.8) | copy-start | bytes 786436
  622.7 17.9 %copy-start.7 = (f32[2,64,512]{2,1,0:T(8,128)S(1)}, f32[2,64,512]{2,1,0:T(8,128)}, u32[]{:S(2)}) copy-start(f32[2,64,512]{2,1,0:T(8,128)} %copy-done.6) | copy-start | bytes 786436
  640.9 112.4 %copy-start.5 = (bf16[512,1024]{1,0:T(8,128)(2,1)S(1)}, bf16[512,1024]{1,0:T(8,128)(2,1)}, u32[]{:S(2)}) copy-start(bf16[512,1024]{1,0:T(8,128)(2,1)} %param.3) | copy-start | bytes 3145732
  643.4 199.9 %reduce-scatter.9.cloned.1.call-start = ((), (), s32[]{:S(2)}) async-start(), calls=%async_computation.11 | async-start | bytes 4456448 | tf_op jit(solution)/shard_map/reduce_scatter | solution.py:73
  770.3 86.0 %reduce-scatter.11.cloned.1.call-start = ((), (), s32[]{:S(2)}) async-start(), calls=%async_computation.12 | async-start | bytes 393216 | tf_op jit(solution)/shard_map/reduce_scatter | solution.py:82
Sparse Core Ops, SparseCore 0:
  15.2 102.0 reduce-scatter.4
  121.1 72.7 reduce-scatter.6
  232.9 47.6 all-gather.5
  298.2 48.9 all-gather.7
  365.9 48.9 all-gather.9
  433.4 48.9 all-gather.11
  643.5 101.2 all-gather.13
  770.4 72.7 reduce-scatter.8
  845.5 10.7 reduce-scatter.10
